TPU v7x, 32 devices: a whole 2x2x4 slice. The times are simulated.
32 devices in a mesh: ex: 4 (over y, x), ey: 2 (over core), tp: 4 (over z).
Axes of the slice: x: 2, y: 2, z: 4, core: 2. Of those that a mesh axis runs over, the one named last changes fastest.
Arguments:
- tokens: bfloat16 [256, 7168], P(('ex', 'ey'), 'tp'), may hold values from -6 to 6
- cotangent: bfloat16 [256, 7168], P(('ex', 'ey'), 'tp'), may hold values from -0.59765625 to 0.59765625
- gates: bfloat16 [256, 8], P(('ex', 'ey')), may hold values from 0.049804688 to 1
- expert_ids: int32 [256, 8], P(('ex', 'ey')), may hold values from 0 to 31, all different within a row; in each aligned block of 32 rows (0 to 31, 32 to 63, ...) at most 10 rows name the same one
- saved_gate: bfloat16 [1024, 32, 80], P(None, ('ex', 'ey')), may hold values from -6 to 6
- saved_up: bfloat16 [1024, 32, 80], P(None, ('ex', 'ey')), may hold values from -6 to 6
- w_gate: bfloat16 [32, 7168, 1024], P(('ex', 'ey'), 'tp'), may hold values from -0.1875 to 0.1875
- w_up: bfloat16 [32, 7168, 1024], P(('ex', 'ey'), 'tp'), may hold values from -0.1875 to 0.1875
- w_down: bfloat16 [32, 1024, 7168], P(('ex', 'ey'), None, 'tp'), may hold values from -0.25 to 0.25
Outputs:
- grad_tokens: bfloat16 [256, 7168], P(('ex', 'ey'), 'tp')
- grad_gates: bfloat16 [256, 8], P(('ex', 'ey'))
- grad_w_gate: bfloat16 [32, 7168, 1024], P(('ex', 'ey'), 'tp')
- grad_w_up: bfloat16 [32, 7168, 1024], P(('ex', 'ey'), 'tp')
- grad_w_down: bfloat16 [32, 1024, 7168], P(('ex', 'ey'), None, 'tp')
Inputs may be any that keep to these rules, and one draw needn't show every extreme that they name: `expert_ids`: each row names 8 different experts. The rows of one token group name any one expert at most 10 times, a bound that some block reaches.
All inputs are finite; a program needn't handle non-finite values.
Results may differ from a plain program's by a relative error of at most 0.025.
Values may be sent and summed in bfloat16 or wider, within the bound.
A program may use at most 128 MiB of HBM per device.

v0:
```python
import jax
import jax.numpy as jnp
from jax import lax
from jax.sharding import PartitionSpec as P

EXPERTS = 32
TOP = 8
CAP = 10


def slot_codes(expert_ids, capacity, expert_count):
    tok_rows, top_count = expert_ids.shape
    flat = expert_ids.reshape(-1)
    onehot = (flat[:, None] == jnp.arange(expert_count, dtype=jnp.int32)[None, :]).astype(jnp.int32)
    before = jnp.cumsum(onehot, axis=0) - onehot
    position = jnp.sum(before * onehot, axis=1)
    return (flat * capacity + position).reshape(tok_rows, top_count)


def pre_grads(dh_rows, gate_rows, up_rows):
    dh_wide = dh_rows.astype(jnp.float32)
    act_gate = gate_rows.astype(jnp.float32)
    act_up = up_rows.astype(jnp.float32)
    sigm = jax.nn.sigmoid(act_gate)
    d_gate_pre = (dh_wide * act_up * sigm * (1.0 + act_gate * (1.0 - sigm))).astype(jnp.bfloat16)
    d_up_pre = (dh_wide * act_gate * sigm).astype(jnp.bfloat16)
    return (d_gate_pre, d_up_pre)


def on_device(tokens, cotangent, gates, expert_ids, saved_gate, saved_up, w_gate, w_up, w_down):
    expert_count = EXPERTS
    capacity = CAP
    top_count = TOP
    local_width = tokens.shape[1]
    codes = slot_codes(expert_ids, capacity, expert_count)
    slot_rows = jnp.arange(expert_count * capacity, dtype=jnp.int32)
    tables = [
        (codes[:, k][None, :] == slot_rows[:, None]).astype(jnp.bfloat16) for k in range(top_count)
    ]
    chosen = tables[0]
    send_gate = jnp.dot(tables[0], gates[:, 0:1], preferred_element_type=jnp.float32)
    for k in range(1, top_count):
        chosen = chosen + tables[k]
        send_gate = send_gate + jnp.dot(
            tables[k], gates[:, k : k + 1], preferred_element_type=jnp.float32
        )
    send_x = jnp.dot(chosen, tokens, preferred_element_type=jnp.float32).astype(jnp.bfloat16)
    send_dy = jnp.dot(chosen, cotangent, preferred_element_type=jnp.float32).astype(jnp.bfloat16)
    send_x = send_x.reshape(expert_count, capacity, local_width)
    send_dy = send_dy.reshape(expert_count, capacity, local_width)
    send_gate = send_gate.astype(jnp.bfloat16).reshape(expert_count, capacity, 1)
    recv_x, recv_dy, recv_gate = (
        lax.all_to_all(send_x, ("ex", "ey"), split_axis=0, concat_axis=1, tiled=True),
        lax.all_to_all(send_dy, ("ex", "ey"), split_axis=0, concat_axis=1, tiled=True),
        lax.all_to_all(send_gate, ("ex", "ey"), split_axis=0, concat_axis=1, tiled=True),
    )
    scaled = (recv_gate.astype(jnp.float32) * recv_dy.astype(jnp.float32)).astype(jnp.bfloat16)
    gate_act = saved_gate.astype(jnp.float32)
    hidden = (gate_act * jax.nn.sigmoid(gate_act) * saved_up.astype(jnp.float32)).astype(
        jnp.bfloat16
    )
    out_rows = jnp.einsum("fes,efd->esd", hidden, w_down, preferred_element_type=jnp.float32)
    score_part = jnp.sum(recv_dy.astype(jnp.float32) * out_rows, axis=2).astype(jnp.bfloat16)
    dh_local = lax.psum_scatter(
        jnp.einsum("efd,esd->fes", w_down, scaled, preferred_element_type=jnp.float32).astype(
            jnp.bfloat16
        ),
        "tp",
        scatter_dimension=0,
        tiled=True,
    )
    dh_full, score_parts = (
        lax.all_gather(dh_local, "tp", axis=0, tiled=True),
        lax.all_gather(score_part[None], "tp", axis=0, tiled=True),
    )
    d_gate_pre, d_up_pre = pre_grads(dh_full, saved_gate, saved_up)
    score = jnp.sum(score_parts.astype(jnp.float32), axis=0).astype(jnp.bfloat16)
    dx_rows = jnp.einsum("fes,edf->esd", d_gate_pre, w_gate, preferred_element_type=jnp.float32)
    dx_rows = dx_rows + jnp.einsum(
        "fes,edf->esd", d_up_pre, w_up, preferred_element_type=jnp.float32
    )
    dx_rows = dx_rows.astype(jnp.bfloat16)
    grad_w_gate = jnp.einsum(
        "esd,fes->edf", recv_x, d_gate_pre, preferred_element_type=jnp.float32
    ).astype(jnp.bfloat16)
    grad_w_up = jnp.einsum(
        "esd,fes->edf", recv_x, d_up_pre, preferred_element_type=jnp.float32
    ).astype(jnp.bfloat16)
    grad_w_down = jnp.einsum(
        "fes,esd->efd", hidden, scaled, preferred_element_type=jnp.float32
    ).astype(jnp.bfloat16)
    score_col = score[:, :, None]
    back_dx, back_score = (
        lax.all_to_all(dx_rows, ("ex", "ey"), split_axis=1, concat_axis=0, tiled=True),
        lax.all_to_all(score_col, ("ex", "ey"), split_axis=1, concat_axis=0, tiled=True),
    )
    flat_dx = back_dx.reshape(expert_count * capacity, local_width)
    contract = (((0,), (0,)), ((), ()))
    grad_tokens = lax.dot_general(
        chosen, flat_dx, contract, preferred_element_type=jnp.float32
    ).astype(jnp.bfloat16)
    flat_score = back_score.reshape(expert_count * capacity, 1)
    columns = [
        lax.dot_general(tables[k], flat_score, contract, preferred_element_type=jnp.float32)
        for k in range(top_count)
    ]
    grad_gates = jnp.concatenate(columns, axis=1).astype(jnp.bfloat16)
    return (grad_tokens, grad_gates, grad_w_gate, grad_w_up, grad_w_down)


def solution(mesh):
    in_specs = (
        P(("ex", "ey"), "tp"),
        P(("ex", "ey"), "tp"),
        P(("ex", "ey"), None),
        P(("ex", "ey"), None),
        P(None, ("ex", "ey"), None),
        P(None, ("ex", "ey"), None),
        P(("ex", "ey"), "tp", None),
        P(("ex", "ey"), "tp", None),
        P(("ex", "ey"), None, "tp"),
    )
    out_specs = (
        P(("ex", "ey"), "tp"),
        P(("ex", "ey"), None),
        P(("ex", "ey"), "tp", None),
        P(("ex", "ey"), "tp", None),
        P(("ex", "ey"), None, "tp"),
    )
    return jax.shard_map(
        on_device, mesh=mesh, in_specs=in_specs, out_specs=out_specs, check_vma=False
    )
```

profile of v0, /device:TPU:0, one launch (start us, length us, event | category | flops | bytes accessed | tf_op | source)
XLA Modules:
  0.0 181.6 jit_solution(12350616389639696154)
XLA Ops:
  17.1 5.2 %all-to-all-start = ((bf16[32,10,1]{1,2,0:T(2,128)(2,1)}), bf16[32,10,1]{1,2,0:T(2,128)(2,1)S(1)}, u32[]{:S(2)}, u32[]{:S(2)}) async-start(bf16[32,10,1]{1,2,0:T(2,128)(2,1)} %reshape.205), calls=%async_computation | async-start | bytes 32768 | tf_op jit(solution)/shard_map/all_to_all | solution.py:55
  22.8 1.4 reshape.161
  24.2 2.8 %all-to-all-done = bf16[32,10,1]{1,2,0:T(2,128)(2,1)S(1)} async-done(((bf16[32,10,1]{1,2,0:T(2,128)(2,1)}), bf16[32,10,1]{1,2,0:T(2,128)(2,1)S(1)}, u32[]{:S(2)}, u32[]{:S(2)}) %all-to-all-start) | async-done | bytes 672 | tf_op jit(solution)/shard_map/all_to_all | solution.py:55
  27.0 3.6 %all-to-all-start.1 = ((bf16[32,10,1792]{2,1,0:T(8,128)(2,1)}), bf16[32,10,1792]{2,1,0:T(8,128)(2,1)S(1)}, u32[]{:S(2)}, u32[]{:S(2)}) async-start(bf16[32,10,1792]{2,1,0:T(8,128)(2,1)} %reshape.161), calls=%async_computation.1 | async-start | bytes 3670016 | tf_op jit(solution)/shard_map/all_to_all | solution.py:54
  31.2 1.4 reshape.164
  32.8 21.6 %all-to-all-done.1 = bf16[32,10,1792]{2,1,0:T(8,128)(2,1)S(1)} async-done(((bf16[32,10,1792]{2,1,0:T(8,128)(2,1)}), bf16[32,10,1792]{2,1,0:T(8,128)(2,1)S(1)}, u32[]{:S(2)}, u32[]{:S(2)}) %all-to-all-start.1) | async-done | bytes 1146912 | tf_op jit(solution)/shard_map/all_to_all | solution.py:54
  54.4 4.3 %all-to-all-start.4 = ((bf16[32,10,1792]{2,1,0:T(8,128)(2,1)}), bf16[32,10,1792]{2,1,0:T(8,128)(2,1)}, u32[]{:S(2)}, u32[]{:S(2)}) async-start(bf16[32,10,1792]{2,1,0:T(8,128)(2,1)} %reshape.164), calls=%async_computation.5 | async-start | bytes 3670016 | tf_op jit(solution)/shard_map/all_to_all | solution.py:53
  59.4 1.4 copy-done.3
  61.3 10.6 %fusion.12 = bf16[1024,4,80]{0,2,1:T(8,128)(2,1)} fusion(bf16[4,1024,1792]{2,1,0:T(8,128)(2,1)} %param.17, bf16[4,80,1792]{2,0,1:T(4,128)(2,1)S(1)} %multiply_convert_fusion), kind=kOutput, calls=%fused_computation.28 | convolution fusion | flops 1174732800 | bytes 16482304 | tf_op jit(solution)/shard_map/efd,esd->fes/dot_general | solution.py:65
  72.0 8.7 %fusion.1 = bf16[4,80]{1,0:T(4,128)(2,1)S(1)} fusion(bf16[4,1024,1792]{2,1,0:T(8,128)(2,1)} %param.17, f32[4,80,1792]{2,0,1:T(4,128)} %bitcast.140, bf16[1024,4,80]{0,2,1:T(8,128)(2,1)S(1)} %copy-done.4, bf16[1024,4,80]{0,2,1:T(8,128)(2,1)S(1)} %copy-done.2), kind=kOutput, calls=%fused_computation.16 | convolution fusion | flops 1178173184 | bytes 18285184 | tf_op jit(solution)/shard_map/fes,efd->esd/dot_general | solution.py:62
  80.7 11.3 %all-gather.1 = bf16[4,4,80]{2,1,0:T(4,128)(2,1)S(1)} all-gather(bf16[1,4,80]{2,1,0:T(4,128)(2,1)S(1)} %bitcast.145), channel_id=2, replica_groups=mesh['ex'=4,'ey'=2,'tp'=4] {'tp'}, dimensions={0}, use_global_device_ids=true | all-gather | bytes 3200 | tf_op jit(solution)/shard_map/all_gather | solution.py:74
  92.8 4.0 %all-to-all-start.3 = ((bf16[4,80,1]{0,2,1:T(2,128)(2,1)}), bf16[4,80,1]{0,2,1:T(2,128)(2,1)S(1)}, u32[]{:S(2)}, u32[]{:S(2)}) async-start(bf16[4,80,1]{0,2,1:T(2,128)(2,1)} %copy.77), calls=%async_computation.4 | async-start | bytes 81920 | tf_op jit(solution)/shard_map/all_to_all | solution.py:95
  96.7 7.6 %convolution_convert_fusion = bf16[4,1024,1792]{2,1,0:T(8,128)(2,1)} fusion(bf16[4,80,1792]{2,0,1:T(4,128)(2,1)S(1)} %multiply_convert_fusion, bf16[1024,4,80]{0,2,1:T(8,128)(2,1)S(1)} %copy-done.4, bf16[1024,4,80]{0,2,1:T(8,128)(2,1)S(1)} %copy-done.2), kind=kOutput, calls=%fused_computation | convolution fusion | flops 1184366592 | bytes 17137664 | tf_op jit(solution)/shard_map/fes,esd->efd/dot_general | solution.py:89
  104.3 2.1 %copy.80 = bf16[8,4,10,1792]{3,1,2,0:T(4,128)(2,1)S(1)} copy(bf16[8,4,10,1792]{3,2,1,0:T(8,128)(2,1)} %bitcast.37) | data formatting | bytes 2293760 | tf_op jit(solution)/shard_map/all_to_all | solution.py:53
  108.6 17.0 %all_gather.6 = bf16[1024,4,80]{0,2,1:T(8,128)(2,1)S(1)} all-gather(bf16[256,4,80]{0,2,1:T(8,128)(2,1)} %reduce-scatter.2.cloned.1.call-done), channel_id=1, replica_groups=mesh['ex'=4,'ey'=2,'tp'=4] {'tp'}, dimensions={0}, use_global_device_ids=true | all-gather | bytes 819200 | tf_op jit(solution)/shard_map/all_gather | solution.py:73
  125.6 11.1 %fusion.84 = f32[4,80,1792]{2,1,0:T(8,128)} fusion(bf16[4,1792,1024]{2,1,0:T(8,128)(2,1)} %param.15, bf16[1024,4,80]{0,2,1:T(8,128)(2,1)S(1)} %copy-done.4, bf16[1024,4,80]{0,2,1:T(8,128)(2,1)S(1)} %all_gather.6, bf16[1024,4,80]{0,2,1:T(8,128)(2,1)S(1)} %copy-done.2), kind=kOutput, calls=%fused_computation.133 | convolution fusion | flops 1178664960 | bytes 18939904 | tf_op jit(solution)/shard_map/fes,edf->esd/dot_general | solution.py:78
  136.8 11.4 %fusion = bf16[4,80,1792]{2,1,0:T(8,128)(2,1)} fusion(f32[4,80,1792]{2,1,0:T(8,128)} %fusion.84, bf16[4,1792,1024]{2,1,0:T(8,128)(2,1)} %param.16, bf16[1024,4,80]{0,2,1:T(8,128)(2,1)S(1)} %copy-done.2, bf16[1024,4,80]{0,2,1:T(8,128)(2,1)S(1)} %all_gather.6), kind=kOutput, calls=%fused_computation.5 | convolution fusion | flops 1178173440 | bytes 19431424 | tf_op jit(solution)/shard_map/fes,edf->esd/dot_general | solution.py:79
  148.1 2.9 %copy.74 = bf16[4,80,1792]{2,0,1:T(4,128)(2,1)} copy(bf16[4,80,1792]{2,1,0:T(8,128)(2,1)} %fusion) | data formatting | bytes 2293760 | tf_op jit(solution)/shard_map/convert_element_type | solution.py:82
  151.0 4.5 %all-to-all-start.2 = ((bf16[4,80,1792]{2,0,1:T(4,128)(2,1)}), bf16[4,80,1792]{2,0,1:T(4,128)(2,1)}, u32[]{:S(2)}, u32[]{:S(2)}) async-start(bf16[4,80,1792]{2,0,1:T(4,128)(2,1)} %copy.74), calls=%async_computation.3 | async-start | bytes 2293760 | tf_op jit(solution)/shard_map/all_to_all | solution.py:94
  155.5 7.6 %convolution_convert_fusion.2 = bf16[4,1792,1024]{2,1,0:T(8,128)(2,1)} fusion(bf16[4,80,1792]{2,0,1:T(4,128)(2,1)S(1)} %bitcast.138, bf16[1024,4,80]{0,2,1:T(8,128)(2,1)S(1)} %copy-done.4, bf16[1024,4,80]{0,2,1:T(8,128)(2,1)S(1)} %all_gather.6, bf16[1024,4,80]{0,2,1:T(8,128)(2,1)S(1)} %copy-done.2), kind=kOutput, calls=%fused_computation.2 | convolution fusion | flops 1186004992 | bytes 17793024 | tf_op jit(solution)/shard_map/esd,fes->edf/dot_general | solution.py:83
  163.1 7.6 %convolution_convert_fusion.1 = bf16[4,1792,1024]{2,1,0:T(8,128)(2,1)} fusion(bf16[4,80,1792]{2,0,1:T(4,128)(2,1)S(1)} %bitcast.139, bf16[1024,4,80]{0,2,1:T(8,128)(2,1)S(1)} %copy-done.2, bf16[1024,4,80]{0,2,1:T(8,128)(2,1)S(1)} %all_gather.6), kind=kOutput, calls=%fused_computation.1 | convolution fusion | flops 1184366592 | bytes 17137664 | tf_op jit(solution)/shard_map/esd,fes->edf/dot_general | solution.py:86
  170.7 1.0 all-to-all-done.2
  171.7 1.5 copy.75
  173.7 1.1 convolution_convert_fusion.5
  (63 shorter events, 15.7 us)
Async XLA Ops:
  7.2 15.1 %copy-start = (bf16[32,1792]{1,0:T(8,128)(2,1)S(1)}, bf16[32,1792]{1,0:T(8,128)(2,1)}, u32[]{:S(2)}) copy-start(bf16[32,1792]{1,0:T(8,128)(2,1)} %param.10) | copy-start | bytes 344068
  17.1 10.0 %all-to-all-start = ((bf16[32,10,1]{1,2,0:T(2,128)(2,1)}), bf16[32,10,1]{1,2,0:T(2,128)(2,1)S(1)}, u32[]{:S(2)}, u32[]{:S(2)}) async-start(bf16[32,10,1]{1,2,0:T(2,128)(2,1)} %reshape.205), calls=%async_computation | async-start | bytes 32768 | tf_op jit(solution)/shard_map/all_to_all | solution.py:55
  24.2 6.4 %copy-start.5 = (bf16[32,1792]{1,0:T(8,128)(2,1)S(1)}, bf16[32,1792]{1,0:T(8,128)(2,1)}, u32[]{:S(2)}) copy-start(bf16[32,1792]{1,0:T(8,128)(2,1)} %param.9) | copy-start | bytes 344068
  27.0 27.3 %all-to-all-start.1 = ((bf16[32,10,1792]{2,1,0:T(8,128)(2,1)}), bf16[32,10,1792]{2,1,0:T(8,128)(2,1)S(1)}, u32[]{:S(2)}, u32[]{:S(2)}) async-start(bf16[32,10,1792]{2,1,0:T(8,128)(2,1)} %reshape.161), calls=%async_computation.1 | async-start | bytes 3670016 | tf_op jit(solution)/shard_map/all_to_all | solution.py:54
  54.4 38.4 %all-to-all-start.4 = ((bf16[32,10,1792]{2,1,0:T(8,128)(2,1)}), bf16[32,10,1792]{2,1,0:T(8,128)(2,1)}, u32[]{:S(2)}, u32[]{:S(2)}) async-start(bf16[32,10,1792]{2,1,0:T(8,128)(2,1)} %reshape.164), calls=%async_computation.5 | async-start | bytes 3670016 | tf_op jit(solution)/shard_map/all_to_all | solution.py:53
  58.7 49.9 %reduce-scatter.2.cloned.1.call-start = ((), (), s32[]{:S(2)}) async-start(), calls=%async_computation.6 | async-start | bytes 819200 | tf_op jit(solution)/shard_map/reduce_scatter | solution.py:64
  59.3 1.4 copy-start.3
  61.3 10.7 %copy-start.2 = (bf16[1024,4,80]{0,2,1:T(8,128)(2,1)S(1)}, bf16[1024,4,80]{0,2,1:T(8,128)(2,1)}, u32[]{:S(2)}) copy-start(bf16[1024,4,80]{0,2,1:T(8,128)(2,1)} %param.13) | copy-start | bytes 1966084
  61.3 10.7 %copy-start.4 = (bf16[1024,4,80]{0,2,1:T(8,128)(2,1)S(1)}, bf16[1024,4,80]{0,2,1:T(8,128)(2,1)}, u32[]{:S(2)}) copy-start(bf16[1024,4,80]{0,2,1:T(8,128)(2,1)} %param.14) | copy-start | bytes 1966084
  92.8 13.7 %all-to-all-start.3 = ((bf16[4,80,1]{0,2,1:T(2,128)(2,1)}), bf16[4,80,1]{0,2,1:T(2,128)(2,1)S(1)}, u32[]{:S(2)}, u32[]{:S(2)}) async-start(bf16[4,80,1]{0,2,1:T(2,128)(2,1)} %copy.77), calls=%async_computation.4 | async-start | bytes 81920 | tf_op jit(solution)/shard_map/all_to_all | solution.py:95
  151.0 20.7 %all-to-all-start.2 = ((bf16[4,80,1792]{2,0,1:T(4,128)(2,1)}), bf16[4,80,1792]{2,0,1:T(4,128)(2,1)}, u32[]{:S(2)}, u32[]{:S(2)}) async-start(bf16[4,80,1792]{2,0,1:T(4,128)(2,1)} %copy.74), calls=%async_computation.3 | async-start | bytes 2293760 | tf_op jit(solution)/shard_map/all_to_all | solution.py:94
  173.2 1.5 copy-start.1
Sparse Core Ops, SparseCore 0:
  72.1 24.1 reduce-scatter.1
where the time goes:
time: 182 us
  matrix products  74.8 us (41%)
  blocking collectives  28.3 us (16%)
  waiting for transfers between devices  25.4 us (14%)
  starting transfers between devices  21.6 us (12%)
  local copies, waits for them, and re-layouts  15.9 us (9%)
  between operations  14.3 us (8%)
    all_to_all x1, waiting for transfers between devices, on_device(): lax.all_to_all(send_dy, ('ex', 'ey'), split_axis=0, concat_axis=1, tiled=...  21.6 us
    all_gather x1, blocking collectives, on_device(): lax.all_gather(dh_local, 'tp', axis=0, tiled=True)  17 us
    dot_general x1, matrix products, on_device(): jnp.einsum('fes,edf->esd', d_up_pre, w_up, preferred_element_type=jnp.flo...  11.4 us
    all_gather x1, blocking collectives, on_device(): lax.all_gather(score_part[None], 'tp', axis=0, tiled=True)  11.3 us
    dot_general x1, matrix products, on_device(): jnp.einsum('fes,edf->esd', d_gate_pre, w_gate, preferred_element_type=jnp...  11.1 us
    dot_general x1, matrix products, on_device(): jnp.einsum('efd,esd->fes', w_down, scaled, preferred_element_type=jnp.flo...  10.6 us
    dot_general x1, matrix products, on_device(): jnp.einsum('fes,efd->esd', hidden, w_down, preferred_element_type=jnp.flo...  8.72 us
    dot_general x1, matrix products, on_device(): jnp.einsum('esd,fes->edf', recv_x, d_gate_pre, preferred_element_type=jnp...  7.62 us
  transfers between devices with their start and end apart: 6, of which 3 were waited for; matrix products, arithmetic and copies ran while one was open for 29% of the time, Pallas kernels for 0%

commit v1 on v0

v1 whole, which is shorter than its diff:
```python
import jax
import jax.numpy as jnp
from jax import lax
from jax.sharding import PartitionSpec as P

LANES = 128
GROUP = ("ex", "ey")


def scatter_blocks(blocks, parts):
    if parts > 4:
        got = lax.all_to_all(blocks, "tp", split_axis=0, concat_axis=0, tiled=True)
        return [got[i] for i in range(parts)]
    me = lax.axis_index("tp")
    got = [lax.dynamic_index_in_dim(blocks, me, 0, keepdims=False)]
    for step in range(1, parts):
        piece = lax.dynamic_index_in_dim(blocks, (me + step) % parts, 0, keepdims=False)
        got.append(lax.ppermute(piece, "tp", [(i, (i + step) % parts) for i in range(parts)]))
    return got


def block_sum(terms):
    return sum(term.astype(jnp.float32) for term in terms).astype(jnp.bfloat16)


def gather_pieces(block, parts):
    if parts > 4:
        return [lax.all_gather(block, "tp", axis=0)]
    shifts = [[(i, (i + step) % parts) for i in range(parts)] for step in range(1, parts)]
    return [block] + [lax.ppermute(block, "tp", shift) for shift in shifts]


def in_order(pieces, parts):
    if parts > 4:
        return pieces[0]
    me = lax.axis_index("tp")
    whole = jnp.zeros((parts,) + pieces[0].shape, pieces[0].dtype)
    for step, piece in enumerate(pieces):
        whole = lax.dynamic_update_index_in_dim(whole, piece, (me - step) % parts, 0)
    return whole


def on_device(tokens, cotangent, gates, expert_ids, saved_gate, saved_up, w_gate, w_up, w_down):
    groups = lax.axis_size(GROUP)
    parts = lax.axis_size("tp")
    rows, width = tokens.shape
    top = expert_ids.shape[1]
    hidden_units, local, slots = saved_gate.shape
    capacity = slots // groups
    total = groups * rows
    first = lax.axis_index(GROUP) * local

    extra = jnp.concatenate(
        [gates, expert_ids.astype(jnp.bfloat16), jnp.zeros((rows, LANES - 2 * top), jnp.bfloat16)],
        axis=1,
    )
    packed = jnp.concatenate([cotangent, extra], axis=1)
    packed = lax.all_gather(packed, GROUP, axis=0, tiled=True)
    tokens, packed = lax.optimization_barrier((tokens, packed))
    all_x = lax.all_to_all(
        jnp.broadcast_to(tokens[None], (groups, rows, width)),
        GROUP, split_axis=0, concat_axis=0, tiled=True,
    ).reshape(total, width)
    all_dy = packed[:, :width]
    small = packed[:, width:].astype(jnp.float32).T
    all_gates = small[:top]
    all_ids = small[top : 2 * top].astype(jnp.int32)

    match = all_ids[None] == first + jnp.arange(local, dtype=jnp.int32)[:, None, None]
    named = jnp.sum(match.astype(jnp.float32), axis=1)
    gate_of = jnp.sum(jnp.where(match, all_gates[None], 0.0), axis=1)
    place = jnp.arange(total, dtype=jnp.int32)
    group_of = place // rows
    earlier = (place[:, None] < place[None, :]) & (group_of[:, None] == group_of[None, :])
    position = jnp.dot(
        named.astype(jnp.bfloat16), earlier.astype(jnp.bfloat16), preferred_element_type=jnp.float32
    ).astype(jnp.int32)
    row_of = jnp.where(named > 0, group_of[None] * capacity + position, -1)
    taken = row_of[:, None, :] == jnp.arange(slots, dtype=jnp.int32)[None, :, None]
    chosen = taken.astype(jnp.bfloat16).reshape(local * slots, total)
    gate_rows = jnp.sum(jnp.where(taken, gate_of[:, None, :], 0.0), axis=2, keepdims=True)

    dy_rows = jnp.dot(chosen, all_dy, preferred_element_type=jnp.float32).astype(jnp.bfloat16)
    dy_rows = dy_rows.reshape(local, slots, width)
    halves = 2 if local % 2 == 0 else 1
    each = local // halves
    cuts = [slice(h * each, (h + 1) * each) for h in range(halves)]
    received = []
    for cut in cuts:
        raw = jnp.einsum(
            "erd,efd->erf", dy_rows[cut], w_down[cut], preferred_element_type=jnp.float32
        ).astype(jnp.bfloat16)
        raw = raw.reshape(parts, each * slots // parts, hidden_units)
        received.append(scatter_blocks(raw, parts))

    scaled = (gate_rows * dy_rows.astype(jnp.float32)).astype(jnp.bfloat16)
    act_gate = saved_gate.transpose(1, 2, 0).astype(jnp.float32)
    act_up = saved_up.transpose(1, 2, 0).astype(jnp.float32)
    sigm = jax.nn.sigmoid(act_gate)
    hidden = (act_gate * sigm * act_up).astype(jnp.bfloat16)
    sums = [block_sum(received[0])]
    hidden, scaled, sums[0] = lax.optimization_barrier((hidden, scaled, sums[0]))
    grad_w_down = jnp.einsum(
        "erf,erd->efd", hidden, scaled, preferred_element_type=jnp.float32
    ).astype(jnp.bfloat16)

    for terms in received[1:]:
        terms, grad_w_down = lax.optimization_barrier((terms, grad_w_down))
        sums.append(block_sum(terms))
    gathered = [gather_pieces(block, parts) for block in sums]
    d_gate, d_up, score, dx_rows = [], [], [], []
    for cut, pieces in zip(cuts, gathered):
        if dx_rows:
            pieces, dx_rows[-1] = lax.optimization_barrier((pieces, dx_rows[-1]))
        raw = in_order(pieces, parts).reshape(each, slots, hidden_units).astype(jnp.float32)
        a, u, q = act_gate[cut], act_up[cut], sigm[cut]
        dh = gate_rows[cut] * raw
        part_score = jnp.sum(raw * hidden[cut].astype(jnp.float32), axis=2, keepdims=True)
        part_gate = (dh * u * q * (1.0 + a * (1.0 - q))).astype(jnp.bfloat16)
        part_up = (dh * a * q).astype(jnp.bfloat16)
        part_gate, part_up = lax.optimization_barrier((part_gate, part_up))
        dx = jnp.einsum("erf,edf->erd", part_gate, w_gate[cut], preferred_element_type=jnp.float32)
        dx = dx + jnp.einsum("erf,edf->erd", part_up, w_up[cut], preferred_element_type=jnp.float32)
        dx_rows.append(dx.astype(jnp.bfloat16))
        d_gate.append(part_gate)
        d_up.append(part_up)
        score.append(part_score)
    d_gate, d_up, score, dx_rows = [
        jnp.concatenate(pieces, axis=0) for pieces in (d_gate, d_up, score, dx_rows)
    ]
    dx_rows = dx_rows.reshape(local * slots, width)
    own = jnp.arange(LANES)[None, None, :] == jnp.arange(local)[:, None, None]
    score_cols = jnp.where(own, score, 0.0).astype(jnp.bfloat16).reshape(local * slots, LANES)
    over_rows = (((0,), (0,)), ((), ()))
    back = [
        lax.dot_general(chosen, part, over_rows, preferred_element_type=jnp.float32).astype(
            jnp.bfloat16
        )
        for part in (dx_rows, score_cols)
    ]
    back = jnp.concatenate(back, axis=1).reshape(groups, rows, width + LANES)
    back = lax.all_to_all(back, GROUP, split_axis=0, concat_axis=0, tiled=True)

    x_rows = jnp.dot(chosen, all_x, preferred_element_type=jnp.float32).astype(jnp.bfloat16)
    x_rows = x_rows.reshape(local, slots, width)
    grad_w_gate = jnp.einsum(
        "erd,erf->edf", x_rows, d_gate, preferred_element_type=jnp.float32
    ).astype(jnp.bfloat16)
    grad_w_up = jnp.einsum(
        "erd,erf->edf", x_rows, d_up, preferred_element_type=jnp.float32
    ).astype(jnp.bfloat16)

    grad_tokens = jnp.sum(back[:, :, :width].astype(jnp.float32), axis=0).astype(jnp.bfloat16)
    table = back[:, :, width : width + local].transpose(1, 0, 2).reshape(rows, groups * local)
    picks = expert_ids[:, :, None] == jnp.arange(groups * local, dtype=jnp.int32)[None, None, :]
    grad_gates = jnp.sum(
        jnp.where(picks, table.astype(jnp.float32)[:, None, :], 0.0), axis=2
    ).astype(jnp.bfloat16)
    return (grad_tokens, grad_gates, grad_w_gate, grad_w_up, grad_w_down)


def solution(mesh):
    by_group = P(GROUP, "tp")
    small = P(GROUP, None)
    saved = P(None, GROUP, None)
    wide = P(GROUP, "tp", None)
    down = P(GROUP, None, "tp")
    in_specs = (by_group, by_group, small, small, saved, saved, wide, wide, down)
    out_specs = (by_group, small, wide, wide, down)
    return jax.shard_map(
        on_device, mesh=mesh, in_specs=in_specs, out_specs=out_specs, check_vma=False
    )
```

time: 182 us -> 117 us (0.64)
  waiting for transfers between devices: 25.4 us -> 2.95 us
  matrix products: 74.8 us -> 56.2 us
  blocking collectives: 28.3 us -> 12.3 us
  between operations: 14.3 us -> 1.13 us
  local copies, waits for them, and re-layouts: 15.9 us -> 6.86 us
  other arithmetic: 1.36 us -> 8.98 us
  starting transfers between devices: 21.6 us -> 27.6 us
    all_to_all x5 -> x2, waiting for transfers between devices: 25.4 us -> 0.01 us  [the longest x1 0.01 us: on_device(): lax.all_to_all(jnp.broadcast_to(tokens[None], (groups, rows, width)), GRO...]
    ppermute x0 -> x12, starting transfers between devices: none -> 19.5 us  [the longest x6 9.86 us: scatter_blocks(): lax.ppermute(piece, 'tp', [(i, (i + step) % parts) for i in range(parts)])]
    dot_general x26 -> x14, matrix products: 74.8 us -> 56.2 us  [the longest x2 11.1 us: on_device(): jnp.einsum('erf,edf->erd', part_up, w_up[cut], preferred_element_type=jnp...]
    all_gather x2 -> x1, blocking collectives: 28.3 us -> 12.3 us  [on_device(): packed = lax.all_gather(packed, GROUP, axis=0, tiled=True)]
    all_to_all x5 -> x2, starting transfers between devices: 21.5 us -> 8.07 us  [the longest x1 4.23 us: on_device(): lax.all_to_all(jnp.broadcast_to(tokens[None], (groups, rows, width)), GRO...]
    convert_element_type x4 -> x9, other arithmetic: 0.6 us -> 5 us  [the longest x2 1.98 us: block_sum(): sum((term.astype(jnp.float32) for term in terms)).astype(jnp.bfloat16)]
    reshape x4 -> x0, local copies, waits for them, and re-layouts: 4.02 us -> none  [the longest x1 1.43 us: on_device(): send_x = send_x.reshape(expert_count, capacity, local_width)]
    all_to_all x6 -> x0, local copies, waits for them, and re-layouts: 3.75 us -> none  [the longest x1 2.09 us: on_device(): lax.all_to_all(send_x, ('ex', 'ey'), split_axis=0, concat_axis=1, tiled=T...]
  transfers between devices with their start and end apart: 6 -> 14, of which waited for: 3 -> 2; matrix products, arithmetic and copies ran while one was open for 29% -> 57% of each run, Pallas kernels for 0% -> 0%
where the time goes in v1:
time: 117 us; the launch traced here: 116 us
  matrix products  56.2 us (48%)
  starting transfers between devices  27.6 us (24%)
  blocking collectives  12.3 us (11%)
  other arithmetic  8.98 us (8%)
  local copies, waits for them, and re-layouts  6.86 us (6%)
  waiting for transfers between devices  2.95 us (3%)
    all_gather x1, blocking collectives, on_device(): packed = lax.all_gather(packed, GROUP, axis=0, tiled=True)  12.3 us
    dot_general x2, matrix products, on_device(): jnp.einsum('erf,edf->erd', part_up, w_up[cut], preferred_element_type=jnp...  11.1 us
    dot_general x2, matrix products, on_device(): jnp.einsum('erd,efd->erf', dy_rows[cut], w_down[cut], preferred_element_t...  10.9 us
    ppermute x6, starting transfers between devices, scatter_blocks(): lax.ppermute(piece, 'tp', [(i, (i + step) % parts) for i in range(parts)])  9.86 us
    ppermute x6, starting transfers between devices, gather_pieces(): return [block] + [lax.ppermute(block, 'tp', shift) for shift in shifts]  9.63 us
    dot_general x2, matrix products, on_device(): jnp.einsum('erf,edf->erd', part_gate, w_gate[cut], preferred_element_type...  7.96 us
    dot_general x1, matrix products, on_device(): jnp.einsum('erd,erf->edf', x_rows, d_gate, preferred_element_type=jnp.flo...  7.59 us
    dot_general x1, matrix products, on_device(): jnp.einsum('erf,erd->efd', hidden, scaled, preferred_element_type=jnp.flo...  7.57 us
  transfers between devices with their start and end apart: 14, of which 2 were waited for; matrix products, arithmetic and copies ran while one was open for 57% of the time, Pallas kernels for 0%

profile of v1, /device:TPU:0, one launch (start us, length us, event | category | flops | bytes accessed | tf_op | source)
XLA Modules:
  0.0 115.9 jit_solution(15923478106026008111)
XLA Ops:
  3.2 12.3 %all_gather.3 = bf16[256,1920]{1,0:T(8,128)(2,1)S(1)} all-gather(bf16[32,1920]{1,0:T(8,128)(2,1)S(1)} %concatenate.18), channel_id=1, replica_groups=mesh['ex'=4,'ey'=2,'tp'=4] {'ex','ey'}, dimensions={0}, use_global_device_ids=true | all-gather | bytes 1105920 | tf_op jit(solution)/shard_map/all_gather | solution.py:58
  16.5 4.2 %all-to-all-start.1 = ((bf16[8,32,1792]{2,1,0:T(8,128)(2,1)}), bf16[8,32,1792]{2,1,0:T(8,128)(2,1)}, u32[]{:S(2)}, u32[]{:S(2)}) async-start(bf16[8,32,1792]{2,1,0:T(8,128)(2,1)} %broadcast_in_dim.141), calls=%async_computation.1 | async-start | bytes 1835008 | tf_op jit(solution)/shard_map/all_to_all | solution.py:60
  22.6 5.4 %fusion.26 = bf16[2,80,1024]{2,1,0:T(8,128)(2,1)S(1)} fusion(bf16[2,80,1792]{2,1,0:T(8,128)(2,1)S(1)} %bitcast.106, bf16[4,1024,1792]{2,1,0:T(8,128)(2,1)} %param.17), kind=kOutput, calls=%fused_computation.29 | convolution fusion | flops 587366400 | bytes 8241152 | tf_op jit(solution)/shard_map/erd,efd->erf/dot_general | solution.py:90
  28.8 3.6 %collective-permute-start.2 = (bf16[40,1024]{1,0:T(8,128)(2,1)}, bf16[40,1024]{1,0:T(8,128)(2,1)}, u32[]{:S(2)}, u32[]{:S(2)}) collective-permute-start(bf16[40,1024]{1,0:T(8,128)(2,1)} %get-tuple-element.77), channel_id=1, source_target_pairs={{0,3},{1,0},{2,1},{3,2},{4,7},{5,4},{6,5},{7,6},{8,11},{9,8},{10,9... | collective-permute-start | bytes 245768 | tf_op jit(solution)/shard_map/ppermute | solution.py:18
  32.4 5.5 %fusion.29 = bf16[2,80,1024]{2,1,0:T(8,128)(2,1)S(1)} fusion(bf16[2,80,1792]{2,1,0:T(8,128)(2,1)S(1)} %bitcast.105, bf16[4,1024,1792]{2,1,0:T(8,128)(2,1)} %param.17), kind=kOutput, calls=%fused_computation.30 | convolution fusion | flops 587366400 | bytes 8241152 | tf_op jit(solution)/shard_map/erd,efd->erf/dot_general | solution.py:90
  39.6 2.8 %collective-permute-start.5 = (bf16[40,1024]{1,0:T(8,128)(2,1)}, bf16[40,1024]{1,0:T(8,128)(2,1)}, u32[]{:S(2)}, u32[]{:S(2)}) collective-permute-start(bf16[40,1024]{1,0:T(8,128)(2,1)} %get-tuple-element.82), channel_id=1, source_target_pairs={{0,3},{1,0},{2,1},{3,2},{4,7},{5,4},{6,5},{7,6},{8,11},{9,8},{10,9... | collective-permute-start | bytes 245768 | tf_op jit(solution)/shard_map/ppermute | solution.py:18
  42.4 1.1 collective-permute-start.4
  43.6 1.5 %add_divide_fusion = (f32[4,80,1024]{2,1,0:T(8,128)}, bf16[4,80,1024]{2,1,0:T(8,128)(2,1)S(1)}) fusion(bf16[1024,4,80]{0,2,1:T(8,128)(2,1)S(1)} %copy-done.4, bf16[1024,4,80]{0,2,1:T(8,128)(2,1)S(1)} %copy-done.3), kind=kLoop, calls=%fused_computation.28 | loop fusion | flops 2621440 | bytes 3276800 | tf_op jit(solution)/shard_map/div | solution.py:99
  45.2 1.8 %convert_bitcast_fusion = (f32[4,80,1024]{2,1,0:T(8,128)}, f32[4,80,1024]{2,1,0:T(8,128)}) fusion(bf16[1024,4,80]{0,2,1:T(8,128)(2,1)S(1)} %copy-done.3, bf16[1024,4,80]{0,2,1:T(8,128)(2,1)S(1)} %copy-done.4), kind=kLoop, calls=%fused_computation.25 | loop fusion | flops 655360 | bytes 3932160 | tf_op jit(solution)/shard_map/convert_element_type | solution.py:98
  47.4 1.3 %collective-permute-start = (bf16[40,1024]{1,0:T(8,128)(2,1)}, bf16[40,1024]{1,0:T(8,128)(2,1)S(1)}, u32[]{:S(2)}, u32[]{:S(2)}) collective-permute-start(bf16[40,1024]{1,0:T(8,128)(2,1)} %get-tuple-element.79), channel_id=1, source_target_pairs={{0,1},{1,2},{2,3},{3,0},{4,5},{5,6},{6,7},{7,4},{8,9},{9,10},{10,1... | collective-permute-start | bytes 245768 | tf_op jit(solution)/shard_map/ppermute | solution.py:18
  48.7 1.6 %collective-permute-done.4 = bf16[40,1024]{1,0:T(8,128)(2,1)} collective-permute-done((bf16[40,1024]{1,0:T(8,128)(2,1)}, bf16[40,1024]{1,0:T(8,128)(2,1)}, u32[]{:S(2)}, u32[]{:S(2)}) %collective-permute-start.4) | collective-permute-done | bytes 81952 | tf_op jit(solution)/shard_map/ppermute | solution.py:18
  51.4 2.2 %collective-permute-start.11 = (bf16[40,1024]{1,0:T(8,128)(2,1)S(1)}, bf16[40,1024]{1,0:T(8,128)(2,1)S(1)}, u32[]{:S(2)}, u32[]{:S(2)}) collective-permute-start(bf16[40,1024]{1,0:T(8,128)(2,1)S(1)} %fusion.66), channel_id=1, source_target_pairs={{0,3},{1,0},{2,1},{3,2},{4,7},{5,4},{6,5},{7,6},{8,11},{9,8},{10,9... | collective-permute-start | bytes 245768 | tf_op jit(solution)/shard_map/ppermute | solution.py:30
  53.8 7.6 %convolution_convert_fusion.2 = bf16[4,1024,1792]{2,1,0:T(8,128)(2,1)} fusion(bf16[4,80,1024]{2,1,0:T(8,128)(2,1)S(1)} %get-tuple-element.25, bf16[4,80,1792]{2,1,0:T(8,128)(2,1)S(1)} %fusion.25), kind=kOutput, calls=%fused_computation.2 | convolution fusion | flops 1181745152 | bytes 16482304 | tf_op jit(solution)/shard_map/erf,erd->efd/dot_general | solution.py:103
  62.9 3.4 %collective-permute-start.8 = (bf16[40,1024]{1,0:T(8,128)(2,1)S(1)}, bf16[40,1024]{1,0:T(8,128)(2,1)S(1)}, u32[]{:S(2)}, u32[]{:S(2)}) collective-permute-start(bf16[40,1024]{1,0:T(8,128)(2,1)S(1)} %add_convert_fusion), channel_id=1, source_target_pairs={{0,3},{1,0},{2,1},{3,2},{4,7},{5,4},{6,5},{7,6},{8,11},{9,8},{10,9... | collective-permute-start | bytes 245768 | tf_op jit(solution)/shard_map/ppermute | solution.py:30
  67.3 1.3 %collective-permute-done.9 = bf16[40,1024]{1,0:T(8,128)(2,1)S(1)} collective-permute-done((bf16[40,1024]{1,0:T(8,128)(2,1)S(1)}, bf16[40,1024]{1,0:T(8,128)(2,1)S(1)}, u32[]{:S(2)}, u32[]{:S(2)}) %collective-permute-start.9) | collective-permute-done | bytes 81952 | tf_op jit(solution)/shard_map/ppermute | solution.py:30
  68.5 2.4 %collective-permute-start.6 = (bf16[40,1024]{1,0:T(8,128)(2,1)S(1)}, bf16[40,1024]{1,0:T(8,128)(2,1)S(1)}, u32[]{:S(2)}, u32[]{:S(2)}) collective-permute-start(bf16[40,1024]{1,0:T(8,128)(2,1)S(1)} %add_convert_fusion), channel_id=1, source_target_pairs={{0,1},{1,2},{2,3},{3,0},{4,5},{5,6},{6,7},{7,4},{8,9},{9,10},{10,1... | collective-permute-start | bytes 245768 | tf_op jit(solution)/shard_map/ppermute | solution.py:30
  71.4 5.6 %fusion.4 = f32[2,80,1792]{2,1,0:T(8,128)S(1)} fusion(bf16[2,80,1024]{2,1,0:T(8,128)(2,1)S(1)} %get-tuple-element.33, bf16[4,1792,1024]{2,1,0:T(8,128)(2,1)} %param.16), kind=kOutput, calls=%fused_computation.7 | convolution fusion | flops 587202560 | bytes 8814592 | tf_op jit(solution)/shard_map/erf,edf->erd/dot_general | solution.py:123
  77.0 5.6 %fusion.22 = bf16[2,80,1792]{2,1,0:T(8,128)(2,1)S(1)} fusion(f32[2,80,1792]{2,1,0:T(8,128)S(1)} %fusion.4, bf16[2,80,1024]{2,1,0:T(8,128)(2,1)S(1)} %get-tuple-element.32, bf16[4,1792,1024]{2,1,0:T(8,128)(2,1)} %param.15), kind=kOutput, calls=%fused_computation.22 | convolution fusion | flops 587776000 | bytes 9388032 | tf_op jit(solution)/shard_map/erf,edf->erd/dot_general | solution.py:122
  83.3 5.6 %fusion = f32[2,80,1792]{2,1,0:T(8,128)S(1)} fusion(bf16[2,80,1024]{2,1,0:T(8,128)(2,1)S(1)} %get-tuple-element.40, bf16[4,1792,1024]{2,1,0:T(8,128)(2,1)} %param.16), kind=kOutput, calls=%fused_computation.3 | convolution fusion | flops 587202560 | bytes 8814592 | tf_op jit(solution)/shard_map/erf,edf->erd/dot_general | solution.py:123
  89.0 2.4 %fusion.19 = bf16[2,80,1792]{2,1,0:T(8,128)(2,1)S(1)} fusion(f32[2,80,1792]{2,1,0:T(8,128)S(1)} %fusion, bf16[2,80,1024]{2,1,0:T(8,128)(2,1)S(1)} %get-tuple-element.39, bf16[4,1792,1024]{2,1,0:T(8,128)(2,1)S(1)} %bitcast.115), kind=kOutput, calls=%fused_computation.21 | convolution fusion | flops 587776000 | bytes 9388032 | tf_op jit(solution)/shard_map/erf,edf->erd/dot_general | solution.py:122
  93.4 3.8 %all-to-all-start = ((bf16[8,32,1920]{2,1,0:T(8,128)(2,1)}), bf16[8,32,1920]{2,1,0:T(8,128)(2,1)S(1)}, u32[]{:S(2)}, u32[]{:S(2)}) async-start(bf16[8,32,1920]{2,1,0:T(8,128)(2,1)} %bitcast.34), calls=%async_computation | async-start | bytes 1966080 | tf_op jit(solution)/shard_map/all_to_all | solution.py:142
  97.3 1.6 %convolution_convert_fusion.3 = bf16[320,1792]{1,0:T(8,128)(2,1)S(1)} fusion(pred[320,256]{1,0:T(8,128)(4,1)S(1)} %bitcast.107, bf16[256,1792]{1,0:T(8,128)(2,1)} %bitcast.38), kind=kOutput, calls=%fused_computation.16 | convolution fusion | flops 294174720 | bytes 2146304 | tf_op jit(solution)/shard_map/dot_general | solution.py:144
  98.9 7.6 %convolution_convert_fusion.1 = bf16[4,1792,1024]{2,1,0:T(8,128)(2,1)} fusion(bf16[4,80,1792]{2,1,0:T(8,128)(2,1)S(1)} %bitcast.99, bf16[2,80,1024]{2,1,0:T(8,128)(2,1)S(1)} %get-tuple-element.39, bf16[2,80,1024]{2,1,0:T(8,128)(2,1)S(1)} %get-tuple-element.32), kind=kOutput, calls=%fused_computation.1 | convolution fusion | flops 1182072832 | bytes 16482304 | tf_op jit(solution)/shard_map/erd,erf->edf/dot_general | solution.py:146
  106.5 7.6 %convolution_convert_fusion = bf16[4,1792,1024]{2,1,0:T(8,128)(2,1)} fusion(bf16[4,80,1792]{2,1,0:T(8,128)(2,1)S(1)} %bitcast.100, bf16[2,80,1024]{2,1,0:T(8,128)(2,1)S(1)} %get-tuple-element.40, bf16[2,80,1024]{2,1,0:T(8,128)(2,1)S(1)} %get-tuple-element.33), kind=kOutput, calls=%fused_computation | convolution fusion | flops 1182072832 | bytes 16482304 | tf_op jit(solution)/shard_map/erd,erf->edf/dot_general | solution.py:149
  (89 shorter events, 16.9 us)
Async XLA Ops:
  0.6 14.9 %copy-start.6 = (bf16[32,1792]{1,0:T(8,128)(2,1)S(1)}, bf16[32,1792]{1,0:T(8,128)(2,1)}, u32[]{:S(2)}) copy-start(bf16[32,1792]{1,0:T(8,128)(2,1)} %param.9) | copy-start | bytes 344068
  16.5 76.9 %all-to-all-start.1 = ((bf16[8,32,1792]{2,1,0:T(8,128)(2,1)}), bf16[8,32,1792]{2,1,0:T(8,128)(2,1)}, u32[]{:S(2)}, u32[]{:S(2)}) async-start(bf16[8,32,1792]{2,1,0:T(8,128)(2,1)} %broadcast_in_dim.141), calls=%async_computation.1 | async-start | bytes 1835008 | tf_op jit(solution)/shard_map/all_to_all | solution.py:60
  28.8 32.6 %collective-permute-start.2 = (bf16[40,1024]{1,0:T(8,128)(2,1)}, bf16[40,1024]{1,0:T(8,128)(2,1)}, u32[]{:S(2)}, u32[]{:S(2)}) collective-permute-start(bf16[40,1024]{1,0:T(8,128)(2,1)} %get-tuple-element.77), channel_id=1, source_target_pairs={{0,3},{1,0},{2,1},{3,2},{4,7},{5,4},{6,5},{7,6},{8,11},{9,8},{10,9... | collective-permute-start | bytes 245768 | tf_op jit(solution)/shard_map/ppermute | solution.py:18
  32.4 29.5 %collective-permute-start.1 = (bf16[40,1024]{1,0:T(8,128)(2,1)}, bf16[40,1024]{1,0:T(8,128)(2,1)}, u32[]{:S(2)}, u32[]{:S(2)}) collective-permute-start(bf16[40,1024]{1,0:T(8,128)(2,1)} %get-tuple-element.78), channel_id=1, source_target_pairs={{0,2},{1,3},{2,0},{3,1},{4,6},{5,7},{6,4},{7,5},{8,10},{9,11},{10,... | collective-permute-start | bytes 245768 | tf_op jit(solution)/shard_map/ppermute | solution.py:18
  32.4 11.2 %copy-start.3 = (bf16[1024,4,80]{0,2,1:T(8,128)(2,1)S(1)}, bf16[1024,4,80]{0,2,1:T(8,128)(2,1)}, u32[]{:S(2)}) copy-start(bf16[1024,4,80]{0,2,1:T(8,128)(2,1)} %param.14) | copy-start | bytes 1966084
  32.4 11.2 %copy-start.4 = (bf16[1024,4,80]{0,2,1:T(8,128)(2,1)S(1)}, bf16[1024,4,80]{0,2,1:T(8,128)(2,1)}, u32[]{:S(2)}) copy-start(bf16[1024,4,80]{0,2,1:T(8,128)(2,1)} %param.13) | copy-start | bytes 1966084
  38.6 8.8 %collective-permute-start.3 = (bf16[40,1024]{1,0:T(8,128)(2,1)}, bf16[40,1024]{1,0:T(8,128)(2,1)}, u32[]{:S(2)}, u32[]{:S(2)}) collective-permute-start(bf16[40,1024]{1,0:T(8,128)(2,1)} %get-tuple-element.81), channel_id=1, source_target_pairs={{0,1},{1,2},{2,3},{3,0},{4,5},{5,6},{6,7},{7,4},{8,9},{9,10},{10,1... | collective-permute-start | bytes 245768 | tf_op jit(solution)/shard_map/ppermute | solution.py:18
  39.6 9.1 %collective-permute-start.5 = (bf16[40,1024]{1,0:T(8,128)(2,1)}, bf16[40,1024]{1,0:T(8,128)(2,1)}, u32[]{:S(2)}, u32[]{:S(2)}) collective-permute-start(bf16[40,1024]{1,0:T(8,128)(2,1)} %get-tuple-element.82), channel_id=1, source_target_pairs={{0,3},{1,0},{2,1},{3,2},{4,7},{5,4},{6,5},{7,6},{8,11},{9,8},{10,9... | collective-permute-start | bytes 245768 | tf_op jit(solution)/shard_map/ppermute | solution.py:18
  42.4 7.9 %collective-permute-start.4 = (bf16[40,1024]{1,0:T(8,128)(2,1)}, bf16[40,1024]{1,0:T(8,128)(2,1)}, u32[]{:S(2)}, u32[]{:S(2)}) collective-permute-start(bf16[40,1024]{1,0:T(8,128)(2,1)} %get-tuple-element.83), channel_id=1, source_target_pairs={{0,2},{1,3},{2,0},{3,1},{4,6},{5,7},{6,4},{7,5},{8,10},{9,11},{10,... | collective-permute-start | bytes 245768 | tf_op jit(solution)/shard_map/ppermute | solution.py:18
  47.4 14.4 %collective-permute-start = (bf16[40,1024]{1,0:T(8,128)(2,1)}, bf16[40,1024]{1,0:T(8,128)(2,1)S(1)}, u32[]{:S(2)}, u32[]{:S(2)}) collective-permute-start(bf16[40,1024]{1,0:T(8,128)(2,1)} %get-tuple-element.79), channel_id=1, source_target_pairs={{0,1},{1,2},{2,3},{3,0},{4,5},{5,6},{6,7},{7,4},{8,9},{9,10},{10,1... | collective-permute-start | bytes 245768 | tf_op jit(solution)/shard_map/ppermute | solution.py:18
  51.4 10.5 %copy-start.5 = (bf16[40,1024]{1,0:T(8,128)(2,1)S(1)}, bf16[40,1024]{1,0:T(8,128)(2,1)}, u32[]{:S(2)}) copy-start(bf16[40,1024]{1,0:T(8,128)(2,1)} %get-tuple-element.27) | copy-start | bytes 245764
  51.4 19.6 %collective-permute-start.11 = (bf16[40,1024]{1,0:T(8,128)(2,1)S(1)}, bf16[40,1024]{1,0:T(8,128)(2,1)S(1)}, u32[]{:S(2)}, u32[]{:S(2)}) collective-permute-start(bf16[40,1024]{1,0:T(8,128)(2,1)S(1)} %fusion.66), channel_id=1, source_target_pairs={{0,3},{1,0},{2,1},{3,2},{4,7},{5,4},{6,5},{7,6},{8,11},{9,8},{10,9... | collective-permute-start | bytes 245768 | tf_op jit(solution)/shard_map/ppermute | solution.py:30
  53.6 17.3 %collective-permute-start.10 = (bf16[40,1024]{1,0:T(8,128)(2,1)S(1)}, bf16[40,1024]{1,0:T(8,128)(2,1)S(1)}, u32[]{:S(2)}, u32[]{:S(2)}) collective-permute-start(bf16[40,1024]{1,0:T(8,128)(2,1)S(1)} %fusion.66), channel_id=1, source_target_pairs={{0,2},{1,3},{2,0},{3,1},{4,6},{5,7},{6,4},{7,5},{8,10},{9,11},{10,... | collective-permute-start | bytes 245768 | tf_op jit(solution)/shard_map/ppermute | solution.py:30
  53.8 17.2 %copy-start.1 = (f32[4,80,1024]{2,1,0:T(8,128)S(1)}, f32[4,80,1024]{2,1,0:T(8,128)}, u32[]{:S(2)}) copy-start(f32[4,80,1024]{2,1,0:T(8,128)} %get-tuple-element.90) | copy-start | bytes 3932164
  53.8 17.3 %copy-start.2 = (f32[4,80,1024]{2,1,0:T(8,128)S(1)}, f32[4,80,1024]{2,1,0:T(8,128)}, u32[]{:S(2)}) copy-start(f32[4,80,1024]{2,1,0:T(8,128)} %get-tuple-element.91) | copy-start | bytes 3932164
  61.3 9.7 %copy-start = (f32[4,80,1024]{2,1,0:T(8,128)S(1)}, f32[4,80,1024]{2,1,0:T(8,128)}, u32[]{:S(2)}) copy-start(f32[4,80,1024]{2,1,0:T(8,128)} %get-tuple-element.73) | copy-start | bytes 3932164
  61.3 7.2 %collective-permute-start.9 = (bf16[40,1024]{1,0:T(8,128)(2,1)S(1)}, bf16[40,1024]{1,0:T(8,128)(2,1)S(1)}, u32[]{:S(2)}, u32[]{:S(2)}) collective-permute-start(bf16[40,1024]{1,0:T(8,128)(2,1)S(1)} %fusion.66), channel_id=1, source_target_pairs={{0,1},{1,2},{2,3},{3,0},{4,5},{5,6},{6,7},{7,4},{8,9},{9,10},{10,1... | collective-permute-start | bytes 245768 | tf_op jit(solution)/shard_map/ppermute | solution.py:30
  62.9 19.8 %collective-permute-start.8 = (bf16[40,1024]{1,0:T(8,128)(2,1)S(1)}, bf16[40,1024]{1,0:T(8,128)(2,1)S(1)}, u32[]{:S(2)}, u32[]{:S(2)}) collective-permute-start(bf16[40,1024]{1,0:T(8,128)(2,1)S(1)} %add_convert_fusion), channel_id=1, source_target_pairs={{0,3},{1,0},{2,1},{3,2},{4,7},{5,4},{6,5},{7,6},{8,11},{9,8},{10,9... | collective-permute-start | bytes 245768 | tf_op jit(solution)/shard_map/ppermute | solution.py:30
  66.2 16.4 %collective-permute-start.7 = (bf16[40,1024]{1,0:T(8,128)(2,1)S(1)}, bf16[40,1024]{1,0:T(8,128)(2,1)S(1)}, u32[]{:S(2)}, u32[]{:S(2)}) collective-permute-start(bf16[40,1024]{1,0:T(8,128)(2,1)S(1)} %add_convert_fusion), channel_id=1, source_target_pairs={{0,2},{1,3},{2,0},{3,1},{4,6},{5,7},{6,4},{7,5},{8,10},{9,11},{10,... | collective-permute-start | bytes 245768 | tf_op jit(solution)/shard_map/ppermute | solution.py:30
  68.5 14.1 %collective-permute-start.6 = (bf16[40,1024]{1,0:T(8,128)(2,1)S(1)}, bf16[40,1024]{1,0:T(8,128)(2,1)S(1)}, u32[]{:S(2)}, u32[]{:S(2)}) collective-permute-start(bf16[40,1024]{1,0:T(8,128)(2,1)S(1)} %add_convert_fusion), channel_id=1, source_target_pairs={{0,1},{1,2},{2,3},{3,0},{4,5},{5,6},{6,7},{7,4},{8,9},{9,10},{10,1... | collective-permute-start | bytes 245768 | tf_op jit(solution)/shard_map/ppermute | solution.py:30
  71.4 17.5 %slice-start = ((s8[14680064]{0:T(1024)(128)(4,1)}), s8[2097152]{0:T(1024)(128)(4,1)S(1)}, s32[]{:S(2)}) async-start(s8[14680064]{0:T(1024)(128)(4,1)} %bitcast.114), calls=%async_computation.2 | async-start | bytes 4194304
  71.4 17.5 %slice-start.1 = ((s8[14680064]{0:T(1024)(128)(4,1)}), s8[4194304]{0:T(1024)(128)(4,1)S(1)}, s32[]{:S(2)}) async-start(s8[14680064]{0:T(1024)(128)(4,1)} %bitcast.114), calls=%async_computation.3 | async-start | bytes 8388608
  77.0 11.9 %slice-start.2 = ((s8[14680064]{0:T(1024)(128)(4,1)}), s8[4194304]{0:T(1024)(128)(4,1)S(1)}, s32[]{:S(2)}) async-start(s8[14680064]{0:T(1024)(128)(4,1)} %bitcast.114), calls=%async_computation.4 | async-start | bytes 8388608
  93.4 20.7 %all-to-all-start = ((bf16[8,32,1920]{2,1,0:T(8,128)(2,1)}), bf16[8,32,1920]{2,1,0:T(8,128)(2,1)S(1)}, u32[]{:S(2)}, u32[]{:S(2)}) async-start(bf16[8,32,1920]{2,1,0:T(8,128)(2,1)} %bitcast.34), calls=%async_computation | async-start | bytes 1966080 | tf_op jit(solution)/shard_map/all_to_all | solution.py:142
  (1 other events, 5.6 us)
